TPU v7x, 32 devices: a whole 2x2x4 slice. The times are simulated.
32 devices in a mesh: ev: 4 (over y, x), co: 8 (over z, core).
Axes of the slice: x: 2, y: 2, z: 4, core: 2. Of those that a mesh axis runs over, the one named last changes fastest.
Arguments:
- eval_points: float32 [2048, 1024], P('ev', 'co'), may hold values from -7 to 7
- corpus_points: float32 [4096, 1024], P('co', 'ev'), may hold values from -7 to 7
Outputs:
- eval_mapped: float32 [2048, 1024], P(('ev', 'co'))
- corpus_mapped: float32 [4096, 1024], P(('co', 'ev'))
- eval_potential: float32 [2048], P('ev')
- corpus_potential: float32 [4096], P('co')
All inputs are finite; a program needn't handle non-finite values.
Results may differ from a plain program's by a relative error of at most 0.0003.
Values sent between devices are 32-bit elements; how exact they have to be, the bound alone decides.
No kernel may reach another device: no remote copies, remote signals or barrier semaphores. Data moves between devices by JAX's collectives and lax.ppermute only.
A program may use at most 64 MiB of HBM per device.

v0:
```python
import math
import jax
import jax.numpy as jnp
from jax import lax
from jax.sharding import PartitionSpec as P

ITERS = 3
EPSILON = 0.02


def row_reduce(scores):
    largest = lax.pmax(jnp.max(scores, axis=1), "co")
    summed = lax.psum(jnp.sum(jnp.exp(scores - largest[:, None]), axis=1), "co")
    return largest + jnp.log(summed)


def column_reduce(scores):
    largest = lax.pmax(jnp.max(scores, axis=0), "ev")
    summed = lax.psum(jnp.sum(jnp.exp(scores - largest[None, :]), axis=0), "ev")
    return largest + jnp.log(summed)


def on_device(eval_points, corpus_points):
    eval_full = lax.all_gather(eval_points, "co", axis=1, tiled=True)
    corpus_full = lax.all_gather(corpus_points, "ev", axis=1, tiled=True)
    embed_width = eval_full.shape[1]
    eval_rows_here = eval_full.shape[0]
    corpus_rows_here = corpus_full.shape[0]
    eval_norms = jnp.sum(eval_full * eval_full, axis=1)
    corpus_norms = jnp.sum(corpus_full * corpus_full, axis=1)
    cross_term = lax.dot_general(
        eval_full,
        corpus_full,
        (((1,), (1,)), ((), ())),
        precision=lax.Precision.HIGHEST,
        preferred_element_type=jnp.float32,
    )
    cost_tile = (eval_norms[:, None] + corpus_norms[None, :] - 2.0 * cross_term) / embed_width
    log_mass_x = -math.log(eval_rows_here * lax.axis_size("ev"))
    log_mass_y = -math.log(corpus_rows_here * lax.axis_size("co"))
    corpus_potential = jnp.zeros((corpus_rows_here,), jnp.float32)
    eval_potential = jnp.zeros((eval_rows_here,), jnp.float32)
    column_lse = jnp.zeros((corpus_rows_here,), jnp.float32)
    for sweep in range(ITERS):
        eval_potential = EPSILON * log_mass_x - EPSILON * row_reduce(
            (corpus_potential[None, :] - cost_tile) / EPSILON
        )
        column_lse = column_reduce((eval_potential[:, None] - cost_tile) / EPSILON)
        corpus_potential = EPSILON * log_mass_y - EPSILON * column_lse
    row_scores = (corpus_potential[None, :] - cost_tile) / EPSILON
    row_final = row_reduce(row_scores)
    x_weights = jnp.exp(row_scores - row_final[:, None])
    y_weights = jnp.exp((eval_potential[:, None] - cost_tile) / EPSILON - column_lse[None, :])
    eval_portion = eval_rows_here // lax.axis_size("co")
    corpus_portion = corpus_rows_here // lax.axis_size("ev")
    eval_whole = lax.psum(
        jnp.dot(
            x_weights,
            corpus_full,
            precision=lax.Precision.HIGHEST,
            preferred_element_type=jnp.float32,
        ),
        "co",
    )
    eval_mapped = lax.dynamic_slice_in_dim(
        eval_whole, lax.axis_index("co") * eval_portion, eval_portion, 0
    )
    corpus_whole = lax.psum(
        lax.dot_general(
            y_weights,
            eval_full,
            (((0,), (0,)), ((), ())),
            precision=lax.Precision.HIGHEST,
            preferred_element_type=jnp.float32,
        ),
        "ev",
    )
    corpus_mapped = lax.dynamic_slice_in_dim(
        corpus_whole, lax.axis_index("ev") * corpus_portion, corpus_portion, 0
    )
    return (eval_mapped, corpus_mapped, eval_potential, corpus_potential)


def solution(mesh):
    return jax.shard_map(
        on_device,
        mesh=mesh,
        in_specs=(P("ev", "co"), P("co", "ev")),
        out_specs=(P(("ev", "co"), None), P(("co", "ev"), None), P("ev"), P("co")),
        check_vma=False,
    )
```

profile of v0, /device:TPU:0, one launch (start us, length us, event | category | flops | bytes accessed | tf_op | source)
XLA Modules:
  0.0 402.7 jit_solution(11580562035312016209)
XLA Ops:
  7.2 0.0 all-gather.5.cloned.1.call-start
  7.2 0.7 all-gather.5.cloned.1.call-update
  7.9 0.0 all-gather.3.cloned.1.call-start
  7.9 0.7 all-gather.3.cloned.1.call-update
  8.6 0.0 all-reduce.3.cloned.1.call-start
  8.7 38.9 %all-gather.5.cloned.1.call-done = f32[512,1024]{1,0:T(8,128)} async-done(((f32[512,256]{1,0:T(8,128)}), f32[512,1024]{1,0:T(8,128)}) %all-gather.5.cloned.1.call-update) | async-done | bytes 2097168 | tf_op jit(solution)/shard_map/all_gather | solution.py:25
  47.6 1.8 multiply_reduce_fusion
  49.4 30.4 %all-gather.3.cloned.1.call-done = f32[512,1024]{1,0:T(8,128)} async-done(((f32[512,128]{1,0:T(8,128)}), f32[512,1024]{1,0:T(8,128)}) %all-gather.3.cloned.1.call-update) | async-done | bytes 2097168 | tf_op jit(solution)/shard_map/all_gather | solution.py:24
  79.8 0.0 copy-start
  79.8 2.0 multiply_reduce_fusion.1
  81.8 0.3 copy-done
  82.1 5.2 %fusion.8 = (f32[512]{0:T(512)S(1)}, f32[512,512]{0,1:T(8,128)S(1)}) fusion(f32[512,1024]{1,0:T(8,128)S(1)} %copy-done, f32[512,1024]{1,0:T(8,128)} %all-gather.5.cloned.1.call-done, f32[512]{0:T(512)S(1)} %multiply_reduce_fusion, f32[512]{0:T(512)S(1)} %multiply_reduce_fusion.1), kind=kOutput, calls=%fused_computation.25 | convolution fusion | flops 3223059968 | bytes 5249024 | tf_op jit(solution)/shard_map/dot_general | solution.py:31
  87.3 14.5 %pmax.49 = f32[512]{0:T(512)S(1)} all-reduce(f32[512]{0:T(512)S(1)} %get-tuple-element.6), channel_id=1, replica_groups=mesh['ev'=4,'co'=8] {'co'}, use_global_device_ids=true, to_apply=%region_3.0 | all-reduce | flops 512 | bytes 4096 | tf_op jit(solution)/shard_map/pmax | solution.py:12
  101.8 0.2 exponential_reduce_fusion.6
  102.0 13.6 %psum.63 = f32[512]{0:T(512)S(1)} all-reduce(f32[512]{0:T(512)S(1)} %exponential_reduce_fusion.6), channel_id=1, replica_groups=mesh['ev'=4,'co'=8] {'co'}, use_global_device_ids=true, to_apply=%region_5.0 | all-reduce | flops 512 | bytes 4096 | tf_op jit(solution)/shard_map/psum | solution.py:13
  115.6 0.2 fusion.9
  115.8 9.8 %pmax.50 = f32[512]{0:T(512)S(1)} all-reduce(f32[512]{0:T(512)S(1)} %fusion.9), channel_id=1, replica_groups=mesh['ev'=4,'co'=8] {'ev'}, use_global_device_ids=true, to_apply=%region_7.0 | all-reduce | flops 512 | bytes 4096 | tf_op jit(solution)/shard_map/pmax | solution.py:18
  125.6 0.3 exponential_reduce_fusion.5
  125.9 8.0 %psum.64 = f32[512]{0:T(512)S(1)} all-reduce(f32[512]{0:T(512)S(1)} %exponential_reduce_fusion.5), channel_id=1, replica_groups=mesh['ev'=4,'co'=8] {'ev'}, use_global_device_ids=true, to_apply=%region_9.0 | all-reduce | flops 512 | bytes 4096 | tf_op jit(solution)/shard_map/psum | solution.py:19
  134.0 0.2 fusion.10
  134.2 13.6 %pmax.51 = f32[512]{0:T(512)S(1)} all-reduce(f32[512]{0:T(512)S(1)} %fusion.10), channel_id=1, replica_groups=mesh['ev'=4,'co'=8] {'co'}, use_global_device_ids=true, to_apply=%region_11.0 | all-reduce | flops 512 | bytes 4096 | tf_op jit(solution)/shard_map/pmax | solution.py:12
  147.8 0.3 exponential_reduce_fusion.4
  148.1 13.6 %psum.65 = f32[512]{0:T(512)S(1)} all-reduce(f32[512]{0:T(512)S(1)} %exponential_reduce_fusion.4), channel_id=1, replica_groups=mesh['ev'=4,'co'=8] {'co'}, use_global_device_ids=true, to_apply=%region_13.0 | all-reduce | flops 512 | bytes 4096 | tf_op jit(solution)/shard_map/psum | solution.py:13
  161.7 0.2 fusion.11
  161.9 8.9 %pmax.52 = f32[512]{0:T(512)S(1)} all-reduce(f32[512]{0:T(512)S(1)} %fusion.11), channel_id=1, replica_groups=mesh['ev'=4,'co'=8] {'ev'}, use_global_device_ids=true, to_apply=%region_15.0 | all-reduce | flops 512 | bytes 4096 | tf_op jit(solution)/shard_map/pmax | solution.py:18
  170.8 0.3 exponential_reduce_fusion.3
  171.1 8.0 %psum.66 = f32[512]{0:T(512)S(1)} all-reduce(f32[512]{0:T(512)S(1)} %exponential_reduce_fusion.3), channel_id=1, replica_groups=mesh['ev'=4,'co'=8] {'ev'}, use_global_device_ids=true, to_apply=%region_17.0 | all-reduce | flops 512 | bytes 4096 | tf_op jit(solution)/shard_map/psum | solution.py:19
  179.2 0.2 fusion.12
  179.4 13.6 %pmax.53 = f32[512]{0:T(512)S(1)} all-reduce(f32[512]{0:T(512)S(1)} %fusion.12), channel_id=1, replica_groups=mesh['ev'=4,'co'=8] {'co'}, use_global_device_ids=true, to_apply=%region_19.0 | all-reduce | flops 512 | bytes 4096 | tf_op jit(solution)/shard_map/pmax | solution.py:12
  193.0 0.3 exponential_reduce_fusion.2
  193.3 13.6 %psum.67 = f32[512]{0:T(512)S(1)} all-reduce(f32[512]{0:T(512)S(1)} %exponential_reduce_fusion.2), channel_id=1, replica_groups=mesh['ev'=4,'co'=8] {'co'}, use_global_device_ids=true, to_apply=%region_21.0 | all-reduce | flops 512 | bytes 4096 | tf_op jit(solution)/shard_map/psum | solution.py:13
  206.9 0.0 copy-start.1
  206.9 0.2 fusion.13
  207.1 9.7 %pmax.54 = f32[512]{0:T(512)S(1)} all-reduce(f32[512]{0:T(512)S(1)} %fusion.13), channel_id=1, replica_groups=mesh['ev'=4,'co'=8] {'ev'}, use_global_device_ids=true, to_apply=%region_23.0 | all-reduce | flops 512 | bytes 4096 | tf_op jit(solution)/shard_map/pmax | solution.py:18
  216.8 0.3 exponential_reduce_fusion.1
  217.1 8.0 %psum.68 = f32[512]{0:T(512)S(1)} all-reduce(f32[512]{0:T(512)S(1)} %exponential_reduce_fusion.1), channel_id=1, replica_groups=mesh['ev'=4,'co'=8] {'ev'}, use_global_device_ids=true, to_apply=%region_25.0 | all-reduce | flops 512 | bytes 4096 | tf_op jit(solution)/shard_map/psum | solution.py:19
  225.2 0.0 copy-start.2
  225.2 0.2 fusion.14
  225.4 13.6 %pmax.55 = f32[512]{0:T(512)S(1)} all-reduce(f32[512]{0:T(512)S(1)} %fusion.14), channel_id=1, replica_groups=mesh['ev'=4,'co'=8] {'co'}, use_global_device_ids=true, to_apply=%region_27.0 | all-reduce | flops 512 | bytes 4096 | tf_op jit(solution)/shard_map/pmax | solution.py:12
  239.0 0.3 exponential_reduce_fusion
  239.2 13.8 %psum.69 = f32[512]{0:T(512)S(1)} all-reduce(f32[512]{0:T(512)S(1)} %exponential_reduce_fusion), channel_id=1, replica_groups=mesh['ev'=4,'co'=8] {'co'}, use_global_device_ids=true, to_apply=%region_29.0 | all-reduce | flops 512 | bytes 4096 | tf_op jit(solution)/shard_map/psum | solution.py:13
  253.0 6.6 %fusion.5 = f32[512,1024]{1,0:T(8,128)} fusion(f32[512,1024]{1,0:T(8,128)} %all-gather.5.cloned.1.call-done, f32[512,512]{0,1:T(8,128)S(1)} %get-tuple-element.7, f32[512]{0:T(512)S(1)} %log_add_fusion, f32[512]{0:T(512)S(1)} %get-tuple-element.4), kind=kOutput, calls=%fused_computation.8 | convolution fusion | flops 3222011904 | bytes 5246976 | tf_op jit(solution)/shard_map/dot_general | solution.py:57
  259.6 0.0 copy-done.2
  259.6 0.0 all-reduce.3.cloned.1.call-update
  259.6 0.0 all-reduce.5.cloned.1.call-start
  259.7 0.0 copy-done.1
  259.7 5.0 %fusion.2 = f32[512,1024]{1,0:T(8,128)} fusion(f32[512,1024]{1,0:T(8,128)S(1)} %copy-done, f32[512,512]{0,1:T(8,128)S(1)} %get-tuple-element.7, f32[512]{0:T(512)S(1)} %get-tuple-element.5, f32[512]{0:T(512)S(1)} %multiply_subtract_fusion.1), kind=kOutput, calls=%fused_computation.5 | convolution fusion | flops 3222011904 | bytes 5246976 | tf_op jit(solution)/shard_map/dot_general | solution.py:69
  264.7 0.0 all-reduce.5.cloned.1.call-update
  264.7 57.5 %all-reduce.3.cloned.1.call-done = f32[512,1024]{1,0:T(8,128)} async-done(((f32[512,1024]{1,0:T(8,128)}), f32[512,1024]{1,0:T(8,128)}) %all-reduce.3.cloned.1.call-update) | async-done | bytes 2097168 | tf_op jit(solution)/shard_map/psum | solution.py:56
  322.2 1.7 constant_dynamic-slice_fusion.1
  323.9 70.4 %all-reduce.5.cloned.1.call-done = f32[512,1024]{1,0:T(8,128)} async-done(((f32[512,1024]{1,0:T(8,128)}), f32[512,1024]{1,0:T(8,128)}) %all-reduce.5.cloned.1.call-update) | async-done | bytes 2097168 | tf_op jit(solution)/shard_map/psum | solution.py:68
  394.3 1.9 constant_dynamic-slice_fusion
  (7 shorter events, 0.1 us)
Async XLA Ops:
  7.2 40.4 %all-gather.5.cloned.1.call-start = ((), (), s32[]{:S(2)}) async-start(), calls=%async_computation.1 | async-start | bytes 2621440 | tf_op jit(solution)/shard_map/all_gather | solution.py:25
  7.9 71.9 %all-gather.3.cloned.1.call-start = ((), (), s32[]{:S(2)}) async-start(), calls=%async_computation | async-start | bytes 2359296 | tf_op jit(solution)/shard_map/all_gather | solution.py:24
  8.6 313.5 %all-reduce.3.cloned.1.call-start = ((), (), s32[]{:S(2)}) async-start(), calls=%async_computation.2 | async-start | bytes 4194304 | tf_op jit(solution)/shard_map/psum | solution.py:56
  79.8 2.2 copy-start
  206.9 52.8 %copy-start.1 = (f32[512]{0:T(512)}, f32[512]{0:T(512)S(1)}, u32[]{:S(2)}) copy-start(f32[512]{0:T(512)S(1)} %multiply_subtract_fusion.1) | copy-start | bytes 6148
  225.2 34.4 %copy-start.2 = (f32[512]{0:T(512)}, f32[512]{0:T(512)S(1)}, u32[]{:S(2)}) copy-start(f32[512]{0:T(512)S(1)} %get-tuple-element.4) | copy-start | bytes 6148
  259.6 134.6 %all-reduce.5.cloned.1.call-start = ((), (), s32[]{:S(2)}) async-start(), calls=%async_computation.3 | async-start | bytes 4194304 | tf_op jit(solution)/shard_map/psum | solution.py:68
Sparse Core Ops, SparseCore 0:
  9.8 37.7 all-gather.4
  49.2 30.5 all-gather.2
  259.7 62.3 all-reduce.2
  325.1 69.0 all-reduce.4
where the time goes:
time: 403 us
  waiting for transfers between devices  199 us (49%)
  blocking collectives  162 us (40%)
  matrix products  16.8 us (4%)
  between operations  13.8 us (3%)
  other arithmetic  7.07 us (2%)
    psum x1, waiting for transfers between devices, on_device(): lax.psum(lax.dot_general(y_weights, eval_full, (((0,), (0,)), ((), ())),...  70.4 us
    psum x1, waiting for transfers between devices, on_device(): lax.psum(jnp.dot(x_weights, corpus_full, precision=lax.Precision.HIGHEST,...  57.5 us
    pmax x4, blocking collectives, row_reduce(): largest = lax.pmax(jnp.max(scores, axis=1), 'co')  55.3 us
    psum x4, blocking collectives, row_reduce(): summed = lax.psum(jnp.sum(jnp.exp(scores - largest[:, None]), axis=1), 'co')  54.6 us
    all_gather x1, waiting for transfers between devices, on_device(): corpus_full = lax.all_gather(corpus_points, 'ev', axis=1, tiled=True)  38.9 us
    all_gather x1, waiting for transfers between devices, on_device(): eval_full = lax.all_gather(eval_points, 'co', axis=1, tiled=True)  30.4 us
    pmax x3, blocking collectives, column_reduce(): largest = lax.pmax(jnp.max(scores, axis=0), 'ev')  28.4 us
    psum x3, blocking collectives, column_reduce(): summed = lax.psum(jnp.sum(jnp.exp(scores - largest[None, :]), axis=0), 'ev')  24.1 us
  transfers between devices with their start and end apart: 4, of which 4 were waited for; matrix products, arithmetic and copies ran while one was open for 2% of the time, Pallas kernels for 0%

commit v1 on v0

--- a/solution.py
+++ b/solution.py
@@ -3,6 +3,7 @@
 import jax.numpy as jnp
 from jax import lax
 from jax.sharding import PartitionSpec as P
+from jax.lax import axis_index, axis_size, ppermute
 
 ITERS = 3
 EPSILON = 0.02
@@ -21,7 +22,27 @@
 
 
 def on_device(eval_points, corpus_points):
-    eval_full = lax.all_gather(eval_points, "co", axis=1, tiled=True)
+
+    def terms_proceed(target):
+        latest, parts_out, seen_now = (axis_size("co"), axis_index("co"), target.shape[1])
+        vals = tuple((q * latest if nth == 1 else q for nth, q in enumerate(target.shape)))
+        c = 1
+        view_out = lax.dynamic_update_slice_in_dim(
+            jnp.zeros(vals, target.dtype), target, parts_out * seen_now, axis=1
+        )
+        while c < latest:
+            target = ppermute(
+                target,
+                axis_name="co",
+                perm=tuple(((nth, (nth + 1) % latest) for nth in range(latest))),
+            )
+            view_out = lax.dynamic_update_slice_in_dim(
+                view_out, target, (parts_out - c) % latest * seen_now, axis=1
+            )
+            c += 1
+        return view_out
+
+    eval_full = terms_proceed(eval_points)
     corpus_full = lax.all_gather(corpus_points, "ev", axis=1, tiled=True)
     embed_width = eval_full.shape[1]
     eval_rows_here = eval_full.shape[0]

time: 403 us -> 384 us (0.953)
  waiting for transfers between devices: 199 us -> 182 us
    ppermute x0 -> x7, waiting for transfers between devices: none -> 53.4 us  [terms_proceed(): ppermute(target, axis_name='co', perm=tuple(((nth, (nth + 1) % latest) fo...]
    all_gather x1, waiting for transfers between devices: 38.9 us -> 0.02 us  [on_device(): corpus_full = lax.all_gather(corpus_points, 'ev', axis=1, tiled=True)]
    all_gather x1 -> x0, waiting for transfers between devices: 30.4 us -> none  [on_device(): eval_full = lax.all_gather(eval_points, 'co', axis=1, tiled=True)]
  transfers between devices with their start and end apart: 4 -> 10, of which waited for: 4 -> 9; matrix products, arithmetic and copies ran while one was open for 2% -> 2% of each run, Pallas kernels for 0% -> 0%
where the time goes in v1:
time: 384 us
  waiting for transfers between devices  182 us (47%)
  blocking collectives  162 us (42%)
  matrix products  15.3 us (4%)
  between operations  13.9 us (4%)
  other arithmetic  5.48 us (1%)
  local copies, waits for them, and re-layouts  4.3 us (1%)
    psum x1, waiting for transfers between devices, on_device(): lax.psum(lax.dot_general(y_weights, eval_full, (((0,), (0,)), ((), ())),...  70.6 us
    psum x1, waiting for transfers between devices, on_device(): lax.psum(jnp.dot(x_weights, corpus_full, precision=lax.Precision.HIGHEST,...  57.5 us
    psum x4, blocking collectives, row_reduce(): summed = lax.psum(jnp.sum(jnp.exp(scores - largest[:, None]), axis=1), 'co')  54.6 us
    pmax x4, blocking collectives, row_reduce(): largest = lax.pmax(jnp.max(scores, axis=1), 'co')  54.4 us
    ppermute x7, waiting for transfers between devices, terms_proceed(): ppermute(target, axis_name='co', perm=tuple(((nth, (nth + 1) % latest) fo...  53.4 us
    pmax x3, blocking collectives, column_reduce(): largest = lax.pmax(jnp.max(scores, axis=0), 'ev')  29.1 us
    psum x3, blocking collectives, column_reduce(): summed = lax.psum(jnp.sum(jnp.exp(scores - largest[None, :]), axis=0), 'ev')  24.1 us
  transfers between devices with their start and end apart: 10, of which 9 were waited for; matrix products, arithmetic and copies ran while one was open for 2% of the time, Pallas kernels for 0%

profile of v1, /device:TPU:0, one launch (start us, length us, event | category | flops | bytes accessed | tf_op | source)
XLA Modules:
  0.0 383.9 jit_solution(2967165605155588895)
XLA Ops:
  7.2 0.0 copy-start.1
  7.2 0.0 all-gather.2.cloned.1.call-start
  7.2 0.7 all-gather.2.cloned.1.call-update
  7.9 0.0 all-reduce.3.cloned.1.call-start
  8.0 0.5 collective-permute-start
  8.5 8.3 %collective-permute-done = f32[512,128]{1,0:T(8,128)S(1)} collective-permute-done((f32[512,128]{1,0:T(8,128)}, f32[512,128]{1,0:T(8,128)S(1)}, u32[]{:S(2)}, u32[]{:S(2)}) %collective-permute-start) | collective-permute-done | bytes 262176 | tf_op jit(solution)/shard_map/ppermute | solution.py:34
  16.8 0.0 collective-permute-start.1
  16.8 7.6 %collective-permute-done.1 = f32[512,128]{1,0:T(8,128)S(1)} collective-permute-done((f32[512,128]{1,0:T(8,128)S(1)}, f32[512,128]{1,0:T(8,128)S(1)}, u32[]{:S(2)}, u32[]{:S(2)}) %collective-permute-start.1) | collective-permute-done | bytes 262176 | tf_op jit(solution)/shard_map/ppermute | solution.py:34
  24.4 0.0 collective-permute-start.2
  24.4 7.6 %collective-permute-done.2 = f32[512,128]{1,0:T(8,128)S(1)} collective-permute-done((f32[512,128]{1,0:T(8,128)S(1)}, f32[512,128]{1,0:T(8,128)S(1)}, u32[]{:S(2)}, u32[]{:S(2)}) %collective-permute-start.2) | collective-permute-done | bytes 262176 | tf_op jit(solution)/shard_map/ppermute | solution.py:34
  32.0 0.0 collective-permute-start.3
  32.0 7.6 %collective-permute-done.3 = f32[512,128]{1,0:T(8,128)S(1)} collective-permute-done((f32[512,128]{1,0:T(8,128)S(1)}, f32[512,128]{1,0:T(8,128)S(1)}, u32[]{:S(2)}, u32[]{:S(2)}) %collective-permute-start.3) | collective-permute-done | bytes 262176 | tf_op jit(solution)/shard_map/ppermute | solution.py:34
  39.6 0.0 copy-done.2
  39.6 0.0 collective-permute-start.4
  39.6 0.2 broadcast_in_dim.2
  39.8 0.0 copy-done.1
  39.9 7.3 %collective-permute-done.4 = f32[512,128]{1,0:T(8,128)S(1)} collective-permute-done((f32[512,128]{1,0:T(8,128)S(1)}, f32[512,128]{1,0:T(8,128)S(1)}, u32[]{:S(2)}, u32[]{:S(2)}) %collective-permute-start.4) | collective-permute-done | bytes 262176 | tf_op jit(solution)/shard_map/ppermute | solution.py:34
  47.2 0.0 collective-permute-start.5
  47.3 0.0 copy-done.3
  47.3 7.5 %collective-permute-done.5 = f32[512,128]{1,0:T(8,128)S(1)} collective-permute-done((f32[512,128]{1,0:T(8,128)S(1)}, f32[512,128]{1,0:T(8,128)S(1)}, u32[]{:S(2)}, u32[]{:S(2)}) %collective-permute-start.5) | collective-permute-done | bytes 262176 | tf_op jit(solution)/shard_map/ppermute | solution.py:34
  54.8 0.0 collective-permute-start.6
  54.9 7.5 %collective-permute-done.6 = f32[512,128]{1,0:T(8,128)S(1)} collective-permute-done((f32[512,128]{1,0:T(8,128)S(1)}, f32[512,128]{1,0:T(8,128)S(1)}, u32[]{:S(2)}, u32[]{:S(2)}) %collective-permute-start.6) | collective-permute-done | bytes 262176 | tf_op jit(solution)/shard_map/ppermute | solution.py:34
  62.4 0.2 multiply_reduce_fusion.1
  62.7 0.0 all-gather.2.cloned.1.call-done
  62.7 0.0 copy-start
  62.7 2.0 multiply_reduce_fusion
  64.6 0.3 copy-done
  64.9 3.7 fusion.6
  68.7 13.6 %pmax.49 = f32[512]{0:T(512)S(1)} all-reduce(f32[512]{0:T(512)S(1)} %get-tuple-element.6), channel_id=1, replica_groups=mesh['ev'=4,'co'=8] {'co'}, use_global_device_ids=true, to_apply=%region_3.4 | all-reduce | flops 512 | bytes 4096 | tf_op jit(solution)/shard_map/pmax | solution.py:13
  82.2 0.2 exponential_reduce_fusion.6
  82.5 13.6 %psum.63 = f32[512]{0:T(512)S(1)} all-reduce(f32[512]{0:T(512)S(1)} %exponential_reduce_fusion.6), channel_id=1, replica_groups=mesh['ev'=4,'co'=8] {'co'}, use_global_device_ids=true, to_apply=%region_5.6 | all-reduce | flops 512 | bytes 4096 | tf_op jit(solution)/shard_map/psum | solution.py:14
  96.1 0.2 fusion.7
  96.3 10.4 %pmax.50 = f32[512]{0:T(512)S(1)} all-reduce(f32[512]{0:T(512)S(1)} %fusion.7), channel_id=1, replica_groups=mesh['ev'=4,'co'=8] {'ev'}, use_global_device_ids=true, to_apply=%region_7.8 | all-reduce | flops 512 | bytes 4096 | tf_op jit(solution)/shard_map/pmax | solution.py:19
  106.7 0.3 exponential_reduce_fusion.5
  107.0 8.0 %psum.64 = f32[512]{0:T(512)S(1)} all-reduce(f32[512]{0:T(512)S(1)} %exponential_reduce_fusion.5), channel_id=1, replica_groups=mesh['ev'=4,'co'=8] {'ev'}, use_global_device_ids=true, to_apply=%region_9.10 | all-reduce | flops 512 | bytes 4096 | tf_op jit(solution)/shard_map/psum | solution.py:20
  115.0 0.2 fusion.8
  115.2 13.6 %pmax.51 = f32[512]{0:T(512)S(1)} all-reduce(f32[512]{0:T(512)S(1)} %fusion.8), channel_id=1, replica_groups=mesh['ev'=4,'co'=8] {'co'}, use_global_device_ids=true, to_apply=%region_11.12 | all-reduce | flops 512 | bytes 4096 | tf_op jit(solution)/shard_map/pmax | solution.py:13
  128.8 0.3 exponential_reduce_fusion.4
  129.1 13.6 %psum.65 = f32[512]{0:T(512)S(1)} all-reduce(f32[512]{0:T(512)S(1)} %exponential_reduce_fusion.4), channel_id=1, replica_groups=mesh['ev'=4,'co'=8] {'co'}, use_global_device_ids=true, to_apply=%region_13.14 | all-reduce | flops 512 | bytes 4096 | tf_op jit(solution)/shard_map/psum | solution.py:14
  142.7 0.2 fusion.9
  142.9 9.0 %pmax.52 = f32[512]{0:T(512)S(1)} all-reduce(f32[512]{0:T(512)S(1)} %fusion.9), channel_id=1, replica_groups=mesh['ev'=4,'co'=8] {'ev'}, use_global_device_ids=true, to_apply=%region_15.16 | all-reduce | flops 512 | bytes 4096 | tf_op jit(solution)/shard_map/pmax | solution.py:19
  151.9 0.3 exponential_reduce_fusion.3
  152.2 8.0 %psum.66 = f32[512]{0:T(512)S(1)} all-reduce(f32[512]{0:T(512)S(1)} %exponential_reduce_fusion.3), channel_id=1, replica_groups=mesh['ev'=4,'co'=8] {'ev'}, use_global_device_ids=true, to_apply=%region_17.18 | all-reduce | flops 512 | bytes 4096 | tf_op jit(solution)/shard_map/psum | solution.py:20
  160.3 0.2 fusion.10
  160.5 13.6 %pmax.53 = f32[512]{0:T(512)S(1)} all-reduce(f32[512]{0:T(512)S(1)} %fusion.10), channel_id=1, replica_groups=mesh['ev'=4,'co'=8] {'co'}, use_global_device_ids=true, to_apply=%region_19.20 | all-reduce | flops 512 | bytes 4096 | tf_op jit(solution)/shard_map/pmax | solution.py:13
  174.0 0.3 exponential_reduce_fusion.2
  174.3 13.6 %psum.67 = f32[512]{0:T(512)S(1)} all-reduce(f32[512]{0:T(512)S(1)} %exponential_reduce_fusion.2), channel_id=1, replica_groups=mesh['ev'=4,'co'=8] {'co'}, use_global_device_ids=true, to_apply=%region_21.22 | all-reduce | flops 512 | bytes 4096 | tf_op jit(solution)/shard_map/psum | solution.py:14
  187.9 0.2 fusion.11
  188.1 9.7 %pmax.54 = f32[512]{0:T(512)S(1)} all-reduce(f32[512]{0:T(512)S(1)} %fusion.11), channel_id=1, replica_groups=mesh['ev'=4,'co'=8] {'ev'}, use_global_device_ids=true, to_apply=%region_23.24 | all-reduce | flops 512 | bytes 4096 | tf_op jit(solution)/shard_map/pmax | solution.py:19
  197.8 0.3 exponential_reduce_fusion.1
  198.2 8.0 %psum.68 = f32[512]{0:T(512)S(1)} all-reduce(f32[512]{0:T(512)S(1)} %exponential_reduce_fusion.1), channel_id=1, replica_groups=mesh['ev'=4,'co'=8] {'ev'}, use_global_device_ids=true, to_apply=%region_25.26 | all-reduce | flops 512 | bytes 4096 | tf_op jit(solution)/shard_map/psum | solution.py:20
  206.2 0.2 fusion.12
  206.4 13.6 %pmax.55 = f32[512]{0:T(512)S(1)} all-reduce(f32[512]{0:T(512)S(1)} %fusion.12), channel_id=1, replica_groups=mesh['ev'=4,'co'=8] {'co'}, use_global_device_ids=true, to_apply=%region_27.28 | all-reduce | flops 512 | bytes 4096 | tf_op jit(solution)/shard_map/pmax | solution.py:13
  220.0 0.3 exponential_reduce_fusion
  220.3 13.8 %psum.69 = f32[512]{0:T(512)S(1)} all-reduce(f32[512]{0:T(512)S(1)} %exponential_reduce_fusion), channel_id=1, replica_groups=mesh['ev'=4,'co'=8] {'co'}, use_global_device_ids=true, to_apply=%region_29.30 | all-reduce | flops 512 | bytes 4096 | tf_op jit(solution)/shard_map/psum | solution.py:14
  234.1 6.6 %fusion.3 = f32[512,1024]{1,0:T(8,128)} fusion(f32[512,1024]{1,0:T(8,128)} %all-gather.2.cloned.1.call-done, f32[512,512]{0,1:T(8,128)S(1)} %get-tuple-element.7, f32[512]{0:T(512)S(1)} %log_add_fusion, f32[512]{0:T(512)S(1)} %get-tuple-element.4), kind=kOutput, calls=%fused_computation.6 | convolution fusion | flops 3222011904 | bytes 5246976 | tf_op jit(solution)/shard_map/dot_general | solution.py:78
  240.7 0.0 all-reduce.3.cloned.1.call-update
  240.7 0.0 all-reduce.5.cloned.1.call-start
  240.8 5.0 %fusion = f32[512,1024]{1,0:T(8,128)} fusion(f32[512,1024]{1,0:T(8,128)S(1)} %constant_dynamic-update-slice_fusion, f32[512,512]{0,1:T(8,128)S(1)} %get-tuple-element.7, f32[512]{0:T(512)S(1)} %get-tuple-element.5, f32[512]{0:T(512)S(1)} %multiply_subtract_fusion.1), kind=kOutput, calls=%fused_computation.3 | convolution fusion | flops 3222011904 | bytes 5246976 | tf_op jit(solution)/shard_map/dot_general | solution.py:90
  245.7 0.0 all-reduce.5.cloned.1.call-update
  245.8 57.5 %all-reduce.3.cloned.1.call-done = f32[512,1024]{1,0:T(8,128)} async-done(((f32[512,1024]{1,0:T(8,128)}), f32[512,1024]{1,0:T(8,128)}) %all-reduce.3.cloned.1.call-update) | async-done | bytes 2097168 | tf_op jit(solution)/shard_map/psum | solution.py:77
  303.2 1.7 constant_dynamic-slice_fusion.1
  304.9 70.6 %all-reduce.5.cloned.1.call-done = f32[512,1024]{1,0:T(8,128)} async-done(((f32[512,1024]{1,0:T(8,128)}), f32[512,1024]{1,0:T(8,128)}) %all-reduce.5.cloned.1.call-update) | async-done | bytes 2097168 | tf_op jit(solution)/shard_map/psum | solution.py:89
  375.5 1.9 constant_dynamic-slice_fusion
  (21 shorter events, 0.3 us)
Async XLA Ops:
  7.2 32.7 %copy-start.1 = (f32[512,128]{1,0:T(8,128)S(1)}, f32[512,128]{1,0:T(8,128)}, u32[]{:S(2)}) copy-start(f32[512,128]{1,0:T(8,128)} %param.2) | copy-start | bytes 786436
  7.2 55.5 %all-gather.2.cloned.1.call-start = ((), (), s32[]{:S(2)}) async-start(), calls=%async_computation | async-start | bytes 2621440 | tf_op jit(solution)/shard_map/all_gather | solution.py:46
  7.9 295.3 %all-reduce.3.cloned.1.call-start = ((), (), s32[]{:S(2)}) async-start(), calls=%async_computation.1 | async-start | bytes 4194304 | tf_op jit(solution)/shard_map/psum | solution.py:77
  8.0 8.8 %collective-permute-start = (f32[512,128]{1,0:T(8,128)}, f32[512,128]{1,0:T(8,128)S(1)}, u32[]{:S(2)}, u32[]{:S(2)}) collective-permute-start(f32[512,128]{1,0:T(8,128)} %param.2), channel_id=1, source_target_pairs={{0,1},{1,2},{2,3},{3,4},{4,5},{5,6},{6,7},{7,0},{8,9},{9,10},{10,1... | collective-permute-start | bytes 786440 | tf_op jit(solution)/shard_map/ppermute | solution.py:34
  16.8 7.6 %collective-permute-start.1 = (f32[512,128]{1,0:T(8,128)S(1)}, f32[512,128]{1,0:T(8,128)S(1)}, u32[]{:S(2)}, u32[]{:S(2)}) collective-permute-start(f32[512,128]{1,0:T(8,128)S(1)} %collective-permute-done), channel_id=1, source_target_pairs={{0,1},{1,2},{2,3},{3,4},{4,5},{5,6},{6,7},{7,0},{8,9},{9,10},{10,1... | collective-permute-start | bytes 786440 | tf_op jit(solution)/shard_map/ppermute | solution.py:34
  24.4 7.6 %collective-permute-start.2 = (f32[512,128]{1,0:T(8,128)S(1)}, f32[512,128]{1,0:T(8,128)S(1)}, u32[]{:S(2)}, u32[]{:S(2)}) collective-permute-start(f32[512,128]{1,0:T(8,128)S(1)} %collective-permute-done.1), channel_id=1, source_target_pairs={{0,1},{1,2},{2,3},{3,4},{4,5},{5,6},{6,7},{7,0},{8,9},{9,10},{10,1... | collective-permute-start | bytes 786440 | tf_op jit(solution)/shard_map/ppermute | solution.py:34
  32.0 7.6 %copy-start.2 = (f32[512,128]{1,0:T(8,128)}, f32[512,128]{1,0:T(8,128)S(1)}, u32[]{:S(2)}) copy-start(f32[512,128]{1,0:T(8,128)S(1)} %collective-permute-done.2) | copy-start | bytes 786436
  32.0 7.6 %collective-permute-start.3 = (f32[512,128]{1,0:T(8,128)S(1)}, f32[512,128]{1,0:T(8,128)S(1)}, u32[]{:S(2)}, u32[]{:S(2)}) collective-permute-start(f32[512,128]{1,0:T(8,128)S(1)} %collective-permute-done.2), channel_id=1, source_target_pairs={{0,1},{1,2},{2,3},{3,4},{4,5},{5,6},{6,7},{7,0},{8,9},{9,10},{10,1... | collective-permute-start | bytes 786440 | tf_op jit(solution)/shard_map/ppermute | solution.py:34
  39.6 7.6 %collective-permute-start.4 = (f32[512,128]{1,0:T(8,128)S(1)}, f32[512,128]{1,0:T(8,128)S(1)}, u32[]{:S(2)}, u32[]{:S(2)}) collective-permute-start(f32[512,128]{1,0:T(8,128)S(1)} %collective-permute-done.3), channel_id=1, source_target_pairs={{0,1},{1,2},{2,3},{3,4},{4,5},{5,6},{6,7},{7,0},{8,9},{9,10},{10,1... | collective-permute-start | bytes 786440 | tf_op jit(solution)/shard_map/ppermute | solution.py:34
  39.6 7.7 %copy-start.3 = (f32[512,128]{1,0:T(8,128)S(1)}, f32[512,128]{1,0:T(8,128)}, u32[]{:S(2)}) copy-start(f32[512,128]{1,0:T(8,128)} %copy-done.2) | copy-start | bytes 786436
  47.2 7.6 %collective-permute-start.5 = (f32[512,128]{1,0:T(8,128)S(1)}, f32[512,128]{1,0:T(8,128)S(1)}, u32[]{:S(2)}, u32[]{:S(2)}) collective-permute-start(f32[512,128]{1,0:T(8,128)S(1)} %collective-permute-done.4), channel_id=1, source_target_pairs={{0,1},{1,2},{2,3},{3,4},{4,5},{5,6},{6,7},{7,0},{8,9},{9,10},{10,1... | collective-permute-start | bytes 786440 | tf_op jit(solution)/shard_map/ppermute | solution.py:34
  54.8 7.6 %collective-permute-start.6 = (f32[512,128]{1,0:T(8,128)S(1)}, f32[512,128]{1,0:T(8,128)S(1)}, u32[]{:S(2)}, u32[]{:S(2)}) collective-permute-start(f32[512,128]{1,0:T(8,128)S(1)} %collective-permute-done.5), channel_id=1, source_target_pairs={{0,1},{1,2},{2,3},{3,4},{4,5},{5,6},{6,7},{7,0},{8,9},{9,10},{10,1... | collective-permute-start | bytes 786440 | tf_op jit(solution)/shard_map/ppermute | solution.py:34
  62.7 2.2 copy-start
  187.9 52.8 %copy-start.4 = (f32[512]{0:T(512)}, f32[512]{0:T(512)S(1)}, u32[]{:S(2)}) copy-start(f32[512]{0:T(512)S(1)} %multiply_subtract_fusion.1) | copy-start | bytes 6148
  206.2 34.4 %copy-start.5 = (f32[512]{0:T(512)}, f32[512]{0:T(512)S(1)}, u32[]{:S(2)}) copy-start(f32[512]{0:T(512)S(1)} %get-tuple-element.4) | copy-start | bytes 6148
  240.7 134.8 %all-reduce.5.cloned.1.call-start = ((), (), s32[]{:S(2)}) async-start(), calls=%async_computation.2 | async-start | bytes 4194304 | tf_op jit(solution)/shard_map/psum | solution.py:89
Sparse Core Ops, SparseCore 0:
  9.8 37.7 all-gather.1
  240.8 62.3 all-reduce.2
  306.3 69.0 all-reduce.4
